TPU v7x, 512 devices: a whole 4x4x16 slice. The times are simulated.
512 devices in a mesh: seq: 32 (over x, y, core), head: 16 (over z).
Axes of the slice: x: 4, y: 4, z: 16, core: 2. Of those that a mesh axis runs over, the one named last changes fastest.
Arguments:
- queries: bfloat16 [65536, 4096], P(('seq', 'head')), may hold values from -6 to 6
- keys: bfloat16 [65536, 4096], P(('seq', 'head')), may hold values from -6 to 6
- values: bfloat16 [65536, 4096], P(('seq', 'head')), may hold values from -60 to 60
- gain: float32 [4096], replicated, may hold values from 0.1 to 1.9
Outputs:
- normed: bfloat16 [65536, 4096], P(('seq', 'head'))
All inputs are finite; a program needn't handle non-finite values.
Results may differ from a plain program's by a relative error of at most 0.015.
Values may be sent and summed in bfloat16 or wider, within the bound.
A program may use at most 64 MiB of HBM per device.

v0:
```python
import jax
import jax.numpy as jnp
from jax import lax
from jax.sharding import PartitionSpec as P

E = 128
HEADS = 32


def per_device(queries, keys, values, gain):
    groups = lax.axis_size("head")
    local_heads = HEADS // groups
    block = queries.shape[0]
    zpos = lax.axis_index("head")
    gpos = lax.axis_index("seq")
    q = queries.reshape(block, HEADS, E)
    k = keys.reshape(block, HEADS, E)
    v = values.reshape(block, HEADS, E)
    own = jnp.einsum("shd,she->hde", k, v, preferred_element_type=jnp.float32)
    own = own.astype(jnp.bfloat16)
    states = lax.all_to_all(
        own.reshape(groups, local_heads, E, E), "head", split_axis=0, concat_axis=0, tiled=True
    ).astype(jnp.float32)
    total = jnp.sum(states, axis=0).astype(jnp.bfloat16)
    totals = lax.all_gather(total, "seq").astype(jnp.float32)
    count = totals.shape[0]
    reached = (jnp.arange(count) < gpos)[:, None, None, None]
    earlier = jnp.sum(jnp.where(reached, totals, 0.0), axis=0)
    entering = earlier[None] + jnp.cumsum(states, axis=0) - states
    entering = entering.astype(jnp.bfloat16)
    state = lax.all_to_all(entering, "head", split_axis=0, concat_axis=0, tiled=True)
    state = state.reshape(HEADS, E, E)
    lower = jnp.tril(jnp.ones((block, block), dtype=bool))
    scores = jnp.einsum("thd,shd->hts", q, k, preferred_element_type=jnp.float32)
    scores = jnp.where(lower[None], scores, 0.0).astype(jnp.bfloat16)
    inner = jnp.einsum("hts,shd->thd", scores, v, preferred_element_type=jnp.float32)
    outer = jnp.einsum("thd,hde->the", q, state, preferred_element_type=jnp.float32)
    home = (inner + outer).astype(jnp.bfloat16).reshape(block, HEADS * E).astype(jnp.float32)
    meansq = jnp.mean(home * home, axis=1, keepdims=True)
    return (home * lax.rsqrt(meansq + 1e-06) * gain[None, :]).astype(jnp.bfloat16)


def solution(mesh):
    return jax.shard_map(
        per_device,
        mesh=mesh,
        in_specs=(
            P(("seq", "head"), None),
            P(("seq", "head"), None),
            P(("seq", "head"), None),
            P(),
        ),
        out_specs=P(("seq", "head"), None),
        check_vma=False,
    )
```

profile of v0, /device:TPU:1, one launch (start us, length us, event | category | flops | bytes accessed | tf_op | source)
XLA Modules:
  0.0 208.1 jit_solution(16825575383389730317)
XLA Ops:
  6.5 0.0 copy-start
  6.5 0.0 copy-start.1
  6.5 0.0 all-gather.3.cloned.1.call-start
  6.5 1.8 copy.17
  8.3 0.0 copy-done.1
  8.3 0.4 convolution_convert_fusion
  8.8 60.9 %all_to_all.10 = bf16[16,2,128,128]{3,2,1,0:T(8,128)(2,1)S(1)} all-to-all(bf16[16,2,128,128]{3,2,1,0:T(8,128)(2,1)S(1)} %bitcast.51), channel_id=1, replica_groups=mesh['seq'=32,'head'=16] {'head'}, dimensions={0} | all-to-all | bytes 2097152 | tf_op jit(solution)/shard_map/all_to_all | solution.py:21
  69.6 0.8 reduce_sum.30
  70.4 0.0 all-gather.3.cloned.1.call-update
  70.4 61.8 %all-gather.3.cloned.1.call-done = bf16[64,128,128]{2,1,0:T(8,128)(2,1)} async-done(((bf16[2,128,128]{2,1,0:T(8,128)(2,1)}), bf16[64,128,128]{2,1,0:T(8,128)(2,1)}) %all-gather.3.cloned.1.call-update) | async-done | bytes 2097168 | tf_op jit(solution)/shard_map/all_gather | solution.py:25
  132.3 2.2 %fusion = f32[2,128,128]{2,1,0:T(8,128)S(1)} fusion(bf16[32,2,128,128]{3,2,1,0:T(8,128)(2,1)} %bitcast.52, pred[32]{0:T(512)(128)(4,1)S(1)} %iota_compare_fusion.1), kind=kLoop, calls=%fused_computation.1 | loop fusion | flops 3112960 | bytes 2228256 | tf_op jit(solution)/shard_map/reduce_sum | solution.py:28
  134.4 1.3 fusion.3
  135.7 0.0 copy-start.2
  135.7 12.2 %all-to-all-start.1 = ((bf16[16,2,128,128]{3,2,1,0:T(8,128)(2,1)}), bf16[16,2,128,128]{3,2,1,0:T(8,128)(2,1)}, u32[]{:S(2)}, u32[]{:S(2)}) async-start(bf16[16,2,128,128]{3,2,1,0:T(8,128)(2,1)} %fusion.3), calls=%async_computation.1 | async-start | bytes 2097152 | tf_op jit(solution)/shard_map/all_to_all | solution.py:31
  148.0 0.0 copy-done
  148.0 0.0 copy-done.2
  148.0 2.5 %fusion.6 = f32[32,128,128]{1,2,0:T(8,128)} fusion(bf16[128,32,128]{0,2,1:T(8,128)(2,1)S(1)} %bitcast.49, pred[128,128]{1,0:T(8,128)(4,1)S(1)} %iota_compare_fusion, bf16[128,4096]{1,0:T(8,128)(2,1)S(1)} %copy-done.2, bf16[128,4096]{1,0:T(8,128)(2,1)S(1)} %copy-done), kind=kOutput, calls=%fused_computation.13 | convolution fusion | flops 269484032 | bytes 5259264 | tf_op jit(solution)/shard_map/hts,shd->thd/dot_general | solution.py:36
  150.5 43.4 %all-to-all-done.1 = bf16[16,2,128,128]{3,2,1,0:T(8,128)(2,1)} async-done(((bf16[16,2,128,128]{3,2,1,0:T(8,128)(2,1)}), bf16[16,2,128,128]{3,2,1,0:T(8,128)(2,1)}, u32[]{:S(2)}, u32[]{:S(2)}) %all-to-all-start.1) | async-done | bytes 1048608 | tf_op jit(solution)/shard_map/all_to_all | solution.py:31
  193.9 2.7 %multiply_reduce_fusion = (f32[128]{0:T(128)S(1)}, f32[128,32,128]{0,2,1:T(8,128)S(1)}) fusion(bf16[32,128,128]{2,1,0:T(8,128)(2,1)} %bitcast.8, f32[32,128,128]{1,2,0:T(8,128)} %fusion.6, bf16[128,4096]{1,0:T(8,128)(2,1)S(1)} %copy-done), kind=kOutput, calls=%fused_computation.9 | convolution fusion | flops 136839040 | bytes 6291968 | tf_op jit(solution)/shard_map/thd,hde->the/dot_general | solution.py:37
  196.6 0.0 copy-start.3
  196.6 1.9 copy.16
  198.4 0.0 copy-done.3
  198.4 2.8 %multiply_convert_fusion = bf16[128,4096]{1,0:T(8,128)(2,1)} fusion(f32[128,4096]{1,0:T(8,128)} %copy.16, f32[4096]{0:T(1024)S(1)} %copy-done.3, f32[128]{0:T(128)S(1)} %add_rsqrt_fusion), kind=kLoop, calls=%fused_computation.8 | loop fusion | flops 1572864 | bytes 3162624 | tf_op jit(solution)/shard_map/convert_element_type | solution.py:40
  (3 shorter events, 0.0 us)
Async XLA Ops:
  6.5 141.4 %copy-start = (bf16[128,4096]{1,0:T(8,128)(2,1)S(1)}, bf16[128,4096]{1,0:T(8,128)(2,1)}, u32[]{:S(2)}) copy-start(bf16[128,4096]{1,0:T(8,128)(2,1)} %param.4) | copy-start | bytes 3145732
  6.5 1.8 copy-start.1
  6.5 125.7 %all-gather.3.cloned.1.call-start = ((), (), s32[]{:S(2)}) async-start(), calls=%async_computation.2 | async-start | bytes 2162688 | tf_op jit(solution)/shard_map/all_gather | solution.py:25
  135.7 12.2 %copy-start.2 = (bf16[128,4096]{1,0:T(8,128)(2,1)S(1)}, bf16[128,4096]{1,0:T(8,128)(2,1)}, u32[]{:S(2)}) copy-start(bf16[128,4096]{1,0:T(8,128)(2,1)} %param.6) | copy-start | bytes 3145732
  135.7 58.2 %all-to-all-start.1 = ((bf16[16,2,128,128]{3,2,1,0:T(8,128)(2,1)}), bf16[16,2,128,128]{3,2,1,0:T(8,128)(2,1)}, u32[]{:S(2)}, u32[]{:S(2)}) async-start(bf16[16,2,128,128]{3,2,1,0:T(8,128)(2,1)} %fusion.3), calls=%async_computation.1 | async-start | bytes 2097152 | tf_op jit(solution)/shard_map/all_to_all | solution.py:31
  196.6 1.9 copy-start.3
Sparse Core Ops, SparseCore 0:
  70.5 61.6 all-gather.2
where the time goes:
time: 212 us; the launch traced here: 208 us
  waiting for transfers between devices  105 us (50%)
  blocking collectives  60.9 us (29%)
  between operations  13.5 us (6%)
  starting transfers between devices  12.2 us (6%)
  other arithmetic  7.12 us (3%)
  matrix products  5.62 us (3%)
  local copies, waits for them, and re-layouts  3.63 us (2%)
    all_gather x1, waiting for transfers between devices, per_device(): totals = lax.all_gather(total, 'seq').astype(jnp.float32)  61.8 us
    all_to_all x1, blocking collectives, per_device(): lax.all_to_all(own.reshape(groups, local_heads, E, E), 'head', split_axis...  60.9 us
    all_to_all x1, waiting for transfers between devices, per_device(): lax.all_to_all(entering, 'head', split_axis=0, concat_axis=0, tiled=True)  43.4 us
    all_to_all x1, starting transfers between devices, per_device(): lax.all_to_all(entering, 'head', split_axis=0, concat_axis=0, tiled=True)  12.2 us
  transfers between devices with their start and end apart: 2, of which 2 were waited for; matrix products, arithmetic and copies ran while one was open for 1% of the time, Pallas kernels for 0%

commit v1 on v0

v1 whole, which is shorter than its diff:
```python
import jax
import jax.numpy as jnp
from jax import lax
from jax.experimental import pallas as pl
from jax.experimental.pallas import tpu as pltpu
from jax.sharding import PartitionSpec as P

E = 128
HEADS = 32
F32 = jnp.float32
BF16 = jnp.bfloat16
MESH = pl.DeviceIdType.MESH


def states_kernel(
    own, out,
    recv1, tot, recv2, tsum, sib, pbuf, recvy, rbuf, recvx, send3, recv3, send4, fin,
    s1, r1, s2, r2, ss, rs, sy, ry, sx, rx, s3, r3, s4, r4,
):
    g = lax.axis_index("seq")
    z = lax.axis_index("head")
    a, b = lax.div(z, 4), lax.rem(z, 4)
    core = lax.rem(g, 2)
    y = lax.rem(lax.div(g, 2), 4)
    x = lax.div(g, 8)
    other = g + 1 - 2 * core

    def step(v, d):
        return lax.rem(v + d, 4)

    def at_b(d):
        return {"seq": g, "head": a * 4 + step(b, d)}

    def at_a(d):
        return {"seq": g, "head": step(a, d) * 4 + b}

    def at_y(d):
        return {"seq": x * 8 + step(y, d) * 2 + core, "head": z}

    def at_x(d):
        return {"seq": step(x, d) * 8 + y * 2 + core, "head": z}

    def copy(src, dst, send, recv, where):
        return pltpu.make_async_remote_copy(
            src_ref=src, dst_ref=dst, send_sem=send, recv_sem=recv,
            device_id=where, device_id_type=MESH,
        )

    started = []

    def start(copies):
        for one in copies:
            one.start()
        started.extend(copies)
        return copies

    def arrive(copies):
        for one in copies:
            one.wait_recv()

    barrier = pltpu.get_barrier_semaphore()
    peers = [f(d) for f in (at_b, at_a, at_y, at_x) for d in (1, 2, 3)]
    peers.append({"seq": other, "head": z})
    for peer in peers:
        pl.semaphore_signal(barrier, inc=1, device_id=peer, device_id_type=MESH)
    pl.semaphore_wait(barrier, len(peers))

    def to_clusters(h):
        return start([
            copy(own.at[pl.ds(8 * step(b, d) + 4 * h, 4)], recv1.at[h, b],
                 s1.at[h, d - 1], r1.at[h, d - 1], at_b(d))
            for d in (1, 3, 2)
        ])

    def cluster_total(h):
        for i in range(4):
            mine = own[8 * b + 4 * h + i]
            recv1[h, b, i] = mine
            total = recv1[h, 0, i].astype(F32)
            for s in range(1, 4):
                total = total + recv1[h, s, i].astype(F32)
            tot[h, i] = total.astype(BF16)
        recv2[h, a] = tot[h, a]
        return start([
            copy(tot.at[h, step(a, d)], recv2.at[h, a],
                 s2.at[h, d - 1], r2.at[h, d - 1], at_a(d))
            for d in (2, 1, 3)
        ])

    def group_total(h):
        total = recv2[h, 0].astype(F32)
        for s in range(1, 4):
            total = total + recv2[h, s].astype(F32)
        tsum[h] = total.astype(BF16)
        return start([copy(tsum.at[h], sib.at[h], ss.at[h], rs.at[h], {"seq": other, "head": z})])

    def chip_total(h):
        both = (tsum[h].astype(F32) + sib[h].astype(F32)).astype(BF16)
        pbuf[h] = both
        recvy[h, y] = both
        return start([
            copy(pbuf.at[h], recvy.at[h, y], sy.at[h, d - 1], ry.at[h, d - 1], at_y(d))
            for d in (2, 1, 3)
        ])

    def row_total(h):
        total = recvy[h, 0].astype(F32)
        for s in range(1, 4):
            total = total + recvy[h, s].astype(F32)
        row = total.astype(BF16)
        rbuf[h] = row
        recvx[h, x] = row
        return start([
            copy(rbuf.at[h], recvx.at[h, x], sx.at[h, d - 1], rx.at[h, d - 1], at_x(d))
            for d in (2, 1, 3)
        ])

    def earlier_groups(h):
        state = jnp.where(core == 1, sib[h].astype(F32), 0.0)
        for s in range(3):
            state = state + jnp.where(s < y, recvy[h, s].astype(F32), 0.0)
        for s in range(3):
            state = state + jnp.where(s < x, recvx[h, s].astype(F32), 0.0)
        for s in range(4):
            send3[h, s] = state.astype(BF16)
            if s < 3:
                state = state + recv2[h, s].astype(F32)
        recv3[h, a] = send3[h, a]
        return start([
            copy(send3.at[h, step(a, d)], recv3.at[h, a],
                 s3.at[h, d - 1], r3.at[h, d - 1], at_a(d))
            for d in (2, 1, 3)
        ])

    def to_blocks(h):
        for i in range(4):
            state = recv3[h, i].astype(F32)
            for s in range(4):
                send4[h, s, i] = state.astype(BF16)
                if s < 3:
                    state = state + recv1[h, s, i].astype(F32)
        mine = pl.ds(8 * b + 4 * h, 4)
        fin[mine] = send4[h, b]
        return start([
            copy(send4.at[h, step(b, d)], fin.at[mine],
                 s4.at[h, d - 1], r4.at[h, d - 1], at_b(d))
            for d in (1, 3, 2)
        ])

    c1 = [to_clusters(0), to_clusters(1)]
    arrive(c1[0])
    c20 = cluster_total(0)
    arrive(c1[1])
    c21 = cluster_total(1)
    arrive(c20)
    cs0 = group_total(0)
    arrive(cs0)
    cy0 = chip_total(0)
    arrive(c21)
    cs1 = group_total(1)
    arrive(cy0)
    cx0 = row_total(0)
    arrive(cs1)
    cy1 = chip_total(1)
    arrive(cx0)
    c30 = earlier_groups(0)
    arrive(cy1)
    cx1 = row_total(1)
    arrive(cx1)
    c31 = earlier_groups(1)
    arrive(c30)
    c40 = to_blocks(0)
    arrive(c31)
    c41 = to_blocks(1)
    arrive(c40)
    arrive(c41)
    for one in started:
        one.wait_send()
    out[...] = fin[...]


def entering_states(own):
    def buf(*lead):
        return pltpu.VMEM((*lead, E, E), BF16)

    dma = pltpu.SemaphoreType.DMA
    three = [dma((2, 3)), dma((2, 3))]
    vmem = pl.BlockSpec(memory_space=pltpu.VMEM)
    return pl.pallas_call(
        states_kernel,
        out_shape=jax.ShapeDtypeStruct((HEADS, E, E), BF16),
        in_specs=[vmem],
        out_specs=vmem,
        scratch_shapes=[
            buf(2, 4, 4), buf(2, 4), buf(2, 4), buf(2), buf(2), buf(2), buf(2, 4), buf(2),
            buf(2, 4), buf(2, 4), buf(2, 4), buf(2, 4, 4), buf(HEADS),
            *three, *three, dma((2,)), dma((2,)), *three, *three, *three, *three,
        ],
        compiler_params=pltpu.CompilerParams(
            collective_id=0, has_side_effects=True, vmem_limit_bytes=40 * 1024 * 1024
        ),
    )(own)


def per_device(queries, keys, values, gain):
    block = queries.shape[0]
    q = queries.reshape(block, HEADS, E)
    k = keys.reshape(block, HEADS, E)
    v = values.reshape(block, HEADS, E)
    own = jnp.einsum("shd,she->hde", k, v, preferred_element_type=F32).astype(BF16)
    state = entering_states(own)
    lower = jnp.tril(jnp.ones((block, block), dtype=bool))
    scores = jnp.einsum("thd,shd->hts", q, k, preferred_element_type=F32)
    scores = jnp.where(lower[None], scores, 0.0).astype(BF16)
    inner = jnp.einsum("hts,shd->thd", scores, v, preferred_element_type=F32)
    outer = jnp.einsum("thd,hde->the", q, state, preferred_element_type=F32)
    home = (inner + outer).astype(BF16).reshape(block, HEADS * E).astype(F32)
    meansq = jnp.mean(home * home, axis=1, keepdims=True)
    return (home * lax.rsqrt(meansq + 1e-06) * gain[None, :]).astype(BF16)


def solution(mesh):
    return jax.shard_map(
        per_device,
        mesh=mesh,
        in_specs=(
            P(("seq", "head"), None),
            P(("seq", "head"), None),
            P(("seq", "head"), None),
            P(),
        ),
        out_specs=P(("seq", "head"), None),
        check_vma=False,
    )
```

time: 212 us -> 105 us (0.50); the launches traced: 208 us -> 105 us
  waiting for transfers between devices: 105 us -> 0 us
  Pallas kernels: 0 us -> 94.9 us
  blocking collectives: 60.9 us -> 0 us
  between operations: 13.5 us -> 0.06 us
  starting transfers between devices: 12.2 us -> 0 us
  other arithmetic: 7.12 us -> 2.87 us
    pallas_call x0 -> x1, Pallas kernels: none -> 94.9 us  [entering_states(): pl.pallas_call(states_kernel, out_shape=jax.ShapeDtypeStruct((HEADS, E, E...]
    all_gather x1 -> x0, waiting for transfers between devices: 61.8 us -> none  [per_device(): totals = lax.all_gather(total, 'seq').astype(jnp.float32)]
    all_to_all x1 -> x0, blocking collectives: 60.9 us -> none  [per_device(): lax.all_to_all(own.reshape(groups, local_heads, E, E), 'head', split_axis...]
    all_to_all x1 -> x0, waiting for transfers between devices: 43.4 us -> none  [per_device(): lax.all_to_all(entering, 'head', split_axis=0, concat_axis=0, tiled=True)]
    all_to_all x1 -> x0, starting transfers between devices: 12.2 us -> none  [per_device(): lax.all_to_all(entering, 'head', split_axis=0, concat_axis=0, tiled=True)]
    reduce_sum x2 -> x0, other arithmetic: 2.94 us -> none  [the longest x1 2.16 us: per_device(): earlier = jnp.sum(jnp.where(reached, totals, 0.0), axis=0)]
  transfers between devices with their start and end apart: 2 -> 0, of which waited for: 2 -> 0; matrix products, arithmetic and copies ran while one was open for 1% -> 0% of each run, Pallas kernels for 0% -> 0%
where the time goes in v1:
time: 105 us
  Pallas kernels  94.9 us (90%)
  matrix products  3.68 us (4%)
  local copies, waits for them, and re-layouts  3.67 us (3%)
  other arithmetic  2.87 us (3%)
    pallas_call x1, Pallas kernels, entering_states(): pl.pallas_call(states_kernel, out_shape=jax.ShapeDtypeStruct((HEADS, E, E...  94.9 us
    convert_element_type x1, other arithmetic, per_device(): return (home * lax.rsqrt(meansq + 1e-06) * gain[None, :]).astype(BF16)  2.85 us
    dot_general x1, matrix products, per_device(): inner = jnp.einsum('hts,shd->thd', scores, v, preferred_element_type=F32)  2.49 us

profile of v1, /device:TPU:1, one launch (start us, length us, event | category | flops | bytes accessed | tf_op | source)
XLA Modules:
  0.0 105.2 jit_solution(14321296749115428320)
XLA Ops:
  0.0 0.0 copy-start
  0.0 0.0 copy-start.2
  0.0 1.8 %copy.12 = bf16[128,4096]{0,1:T(8,128)(2,1)S(1)} copy(bf16[128,4096]{1,0:T(8,128)(2,1)} %param.5) | data formatting | bytes 2097152 | tf_op jit(solution)/shard_map/reshape | solution.py:208
  1.8 0.0 copy-done
  1.8 0.1 copy-done.2
  1.9 2.5 %fusion.2 = f32[32,128,128]{1,2,0:T(8,128)} fusion(bf16[128,32,128]{0,2,1:T(8,128)(2,1)S(1)} %bitcast.43, pred[128,128]{1,0:T(8,128)(4,1)S(1)} %iota_compare_fusion, bf16[128,4096]{1,0:T(8,128)(2,1)S(1)} %copy-done.2, bf16[128,4096]{1,0:T(8,128)(2,1)S(1)} %copy-done), kind=kOutput, calls=%fused_computation.7 | convolution fusion | flops 269484032 | bytes 5259264 | tf_op jit(solution)/shard_map/hts,shd->thd/dot_general | solution.py:215
  4.3 0.0 copy-start.1
  4.3 0.4 convolution_convert_fusion.own
  4.8 94.9 %shard_map.46 = bf16[32,128,128]{2,1,0:T(8,128)(2,1)S(1)} custom-call(bf16[32,128,128]{2,1,0:T(8,128)(2,1)S(1)} %convolution_convert_fusion.own), custom_call_target="tpu_custom_call" | custom-call | tf_op jit(solution)/shard_map/pallas_call | solution.py:189
  99.7 0.0 copy-done.1
  99.7 0.8 multiply_reduce_fusion
  100.5 0.0 copy-start.3
  100.5 1.9 %copy.8 = f32[128,4096]{1,0:T(8,128)} copy(f32[128,4096]{0,1:T(8,128)S(1)} %bitcast.45) | data formatting | bytes 4194304 | tf_op jit(solution)/shard_map/convert_element_type | solution.py:217
  102.3 0.0 copy-done.3
  102.3 2.8 %multiply_convert_fusion = bf16[128,4096]{1,0:T(8,128)(2,1)} fusion(f32[128,4096]{1,0:T(8,128)} %copy.8, f32[4096]{0:T(1024)S(1)} %copy-done.3, f32[128]{0:T(128)S(1)} %add_rsqrt_fusion), kind=kLoop, calls=%fused_computation.2 | loop fusion | flops 1572864 | bytes 3162624 | tf_op jit(solution)/shard_map/convert_element_type | solution.py:219
  (2 shorter events, 0.0 us)
Async XLA Ops:
  0.0 1.8 %copy-start = (bf16[128,4096]{1,0:T(8,128)(2,1)S(1)}, bf16[128,4096]{1,0:T(8,128)(2,1)}, u32[]{:S(2)}) copy-start(bf16[128,4096]{1,0:T(8,128)(2,1)} %param.4) | copy-start | bytes 3145732
  0.0 1.9 %copy-start.2 = (bf16[128,4096]{1,0:T(8,128)(2,1)S(1)}, bf16[128,4096]{1,0:T(8,128)(2,1)}, u32[]{:S(2)}) copy-start(bf16[128,4096]{1,0:T(8,128)(2,1)} %param.6) | copy-start | bytes 3145732
  4.3 95.3 %copy-start.1 = (f32[32,128,128]{1,2,0:T(8,128)S(1)}, f32[32,128,128]{1,2,0:T(8,128)}, u32[]{:S(2)}) copy-start(f32[32,128,128]{1,2,0:T(8,128)} %fusion.2) | copy-start | bytes 6291460
  100.5 1.9 %copy-start.3 = (f32[4096]{0:T(1024)S(1)}, f32[4096]{0:T(1024)}, u32[]{:S(2)}) copy-start(f32[4096]{0:T(1024)} %param.7) | copy-start | bytes 49156

commit v2 on v1

--- a/solution.py
+++ b/solution.py
@@ -12,9 +12,9 @@
 MESH = pl.DeviceIdType.MESH
 
 
-def states_kernel(
-    own, out,
-    recv1, tot, recv2, tsum, sib, pbuf, recvy, rbuf, recvx, send3, recv3, send4, fin,
+def attention_kernel(
+    q_hbm, k_hbm, v_hbm, out, scale,
+    q, k, v, inner, squares, own, load, recv1, tot, recv2, tsum, sib, pbuf, recvy, rbuf, recvx, send3, recv3, send4, fin,
     s1, r1, s2, r2, ss, rs, sy, ry, sx, rx, s3, r3, s4, r4,
 ):
     g = lax.axis_index("seq")
@@ -58,11 +58,72 @@
         for one in copies:
             one.wait_recv()
 
+    loads = [
+        pltpu.make_async_copy(src, dst, load.at[i])
+        for i, (src, dst) in enumerate(((k_hbm, k), (v_hbm, v), (q_hbm, q)))
+    ]
+    for one in loads:
+        one.start()
+
     barrier = pltpu.get_barrier_semaphore()
     peers = [f(d) for f in (at_b, at_a, at_y, at_x) for d in (1, 2, 3)]
     peers.append({"seq": other, "head": z})
     for peer in peers:
         pl.semaphore_signal(barrier, inc=1, device_id=peer, device_id_type=MESH)
+
+    def cols(head):
+        return pl.ds(pl.multiple_of(head * E, E), E)
+
+    def own_states(h):
+        def body(j, carry):
+            for i in range(4):
+                head = 8 * j + 4 * h + i
+                state = lax.dot_general(
+                    k[:, cols(head)], v[:, cols(head)], (((0,), (0,)), ((), ())),
+                    preferred_element_type=F32,
+                )
+                own[head] = state.astype(BF16)
+            return carry
+
+        lax.fori_loop(0, 4, body, 0)
+
+    def inner_products():
+        lower = lax.broadcasted_iota(jnp.int32, (E, E), 0) >= lax.broadcasted_iota(
+            jnp.int32, (E, E), 1
+        )
+
+        def body(j, carry):
+            for i in range(4):
+                at = cols(4 * j + i)
+                scores = lax.dot_general(
+                    q[:, at], k[:, at], (((1,), (1,)), ((), ())), preferred_element_type=F32
+                )
+                scores = jnp.where(lower, scores, 0.0).astype(BF16)
+                inner[:, at] = jnp.dot(scores, v[:, at], preferred_element_type=F32)
+            return carry
+
+        lax.fori_loop(0, HEADS // 4, body, 0)
+        squares[...] = jnp.zeros_like(squares)
+
+    def outer_products(h):
+        def body(j, carry):
+            total = squares[...]
+            for i in range(4):
+                head = 8 * j + 4 * h + i
+                at = cols(head)
+                outer = jnp.dot(q[:, at], fin[head], preferred_element_type=F32)
+                attended = (inner[:, at] + outer).astype(BF16)
+                out[:, at] = attended
+                wide = attended.astype(F32)
+                total = total + wide * wide
+            squares[...] = total
+            return carry
+
+        lax.fori_loop(0, 4, body, 0)
+
+    loads[0].wait()
+    loads[1].wait()
+    own_states(0)
     pl.semaphore_wait(barrier, len(peers))
 
     def to_clusters(h):
@@ -147,7 +208,11 @@
             for d in (1, 3, 2)
         ])
 
-    c1 = [to_clusters(0), to_clusters(1)]
+    c1 = [to_clusters(0)]
+    own_states(1)
+    c1.append(to_clusters(1))
+    loads[2].wait()
+    inner_products()
     arrive(c1[0])
     c20 = cluster_total(0)
     arrive(c1[1])
@@ -173,50 +238,46 @@
     arrive(c31)
     c41 = to_blocks(1)
     arrive(c40)
+    outer_products(0)
     arrive(c41)
+    outer_products(1)
+    meansq = jnp.sum(squares[...], axis=1, keepdims=True) * (1.0 / (HEADS * E))
+    scale[...] = jnp.broadcast_to(lax.rsqrt(meansq + 1e-06), scale.shape)
     for one in started:
         one.wait_send()
-    out[...] = fin[...]
-
-
-def entering_states(own):
+
+
+def per_device(queries, keys, values, gain):
+    rows, feat = queries.shape
+
     def buf(*lead):
         return pltpu.VMEM((*lead, E, E), BF16)
 
     dma = pltpu.SemaphoreType.DMA
     three = [dma((2, 3)), dma((2, 3))]
     vmem = pl.BlockSpec(memory_space=pltpu.VMEM)
-    return pl.pallas_call(
-        states_kernel,
-        out_shape=jax.ShapeDtypeStruct((HEADS, E, E), BF16),
-        in_specs=[vmem],
-        out_specs=vmem,
+    hbm = pl.BlockSpec(memory_space=pltpu.HBM)
+    tokens = pltpu.VMEM((rows, feat), BF16)
+    attended, scale = pl.pallas_call(
+        attention_kernel,
+        out_shape=(
+            jax.ShapeDtypeStruct((rows, feat), BF16),
+            jax.ShapeDtypeStruct((rows, E), F32),
+        ),
+        in_specs=[hbm] * 3,
+        out_specs=(vmem, vmem),
         scratch_shapes=[
+            tokens, tokens, tokens, pltpu.VMEM((rows, feat), F32), pltpu.VMEM((rows, E), F32),
+            buf(HEADS), dma((3,)),
             buf(2, 4, 4), buf(2, 4), buf(2, 4), buf(2), buf(2), buf(2), buf(2, 4), buf(2),
             buf(2, 4), buf(2, 4), buf(2, 4), buf(2, 4, 4), buf(HEADS),
             *three, *three, dma((2,)), dma((2,)), *three, *three, *three, *three,
         ],
         compiler_params=pltpu.CompilerParams(
-            collective_id=0, has_side_effects=True, vmem_limit_bytes=40 * 1024 * 1024
+            collective_id=0, has_side_effects=True, vmem_limit_bytes=65600000
         ),
-    )(own)
-
-
-def per_device(queries, keys, values, gain):
-    block = queries.shape[0]
-    q = queries.reshape(block, HEADS, E)
-    k = keys.reshape(block, HEADS, E)
-    v = values.reshape(block, HEADS, E)
-    own = jnp.einsum("shd,she->hde", k, v, preferred_element_type=F32).astype(BF16)
-    state = entering_states(own)
-    lower = jnp.tril(jnp.ones((block, block), dtype=bool))
-    scores = jnp.einsum("thd,shd->hts", q, k, preferred_element_type=F32)
-    scores = jnp.where(lower[None], scores, 0.0).astype(BF16)
-    inner = jnp.einsum("hts,shd->thd", scores, v, preferred_element_type=F32)
-    outer = jnp.einsum("thd,hde->the", q, state, preferred_element_type=F32)
-    home = (inner + outer).astype(BF16).reshape(block, HEADS * E).astype(F32)
-    meansq = jnp.mean(home * home, axis=1, keepdims=True)
-    return (home * lax.rsqrt(meansq + 1e-06) * gain[None, :]).astype(BF16)
+    )(queries, keys, values)
+    return (attended.astype(F32) * scale[:, :1] * gain[None, :]).astype(BF16)
 
 
 def solution(mesh):

time: 105 us -> 101 us (0.962)
  matrix products: 3.68 us -> 0 us
  local copies, waits for them, and re-layouts: 3.67 us -> 0.95 us
  Pallas kernels: 94.9 us -> 97 us
    dot_general x3 -> x0, matrix products: 3.68 us -> none  [the longest x1 2.49 us: per_device(): inner = jnp.einsum('hts,shd->thd', scores, v, preferred_element_type=F32)]
    pallas_call x1, Pallas kernels: 94.9 us -> 97 us  [per_device(): pl.pallas_call(attention_kernel, out_shape=(jax.ShapeDtypeStruct((rows, f...]
    convert_element_type x1 -> x0, local copies, waits for them, and re-layouts: 1.85 us -> none  [per_device(): home = (inner + outer).astype(BF16).reshape(block, HEADS * E).astype(F32)]
    reshape x1 -> x0, local copies, waits for them, and re-layouts: 1.76 us -> none  [per_device(): k = keys.reshape(block, HEADS, E)]
where the time goes in v2:
time: 101 us
  Pallas kernels  97 us (96%)
  other arithmetic  2.52 us (2%)
    pallas_call x1, Pallas kernels, per_device(): pl.pallas_call(attention_kernel, out_shape=(jax.ShapeDtypeStruct((rows, f...  97 us
    convert_element_type x1, other arithmetic, per_device(): return (attended.astype(F32) * scale[:, :1] * gain[None, :]).astype(BF16)  2.52 us

profile of v2, /device:TPU:1, one launch (start us, length us, event | category | flops | bytes accessed | tf_op | source)
XLA Modules:
  0.0 100.5 jit_solution(17338609669021165389)
XLA Ops:
  0.0 0.0 copy-start
  0.0 97.0 %shard_map.46 = (bf16[128,4096]{1,0:T(8,128)(2,1)}, f32[128,128]{1,0:T(8,128)}) custom-call(bf16[128,4096]{1,0:T(8,128)(2,1)} %q_hbm.1, bf16[128,4096]{1,0:T(8,128)(2,1)} %k_hbm.1, bf16[128,4096]{1,0:T(8,128)(2,1)} %v_hbm.1), custom_call_target="tpu_custom_call" | custom-call | tf_op jit(solution)/shard_map/pallas_call | solution.py:261
  97.0 0.9 slice_reduce_fusion
  98.0 0.0 copy-done
  98.0 2.5 %multiply_convert_fusion = bf16[128,4096]{1,0:T(8,128)(2,1)} fusion(bf16[128,4096]{1,0:T(8,128)(2,1)} %get-tuple-element.7, f32[4096]{0:T(1024)S(1)} %copy-done, f32[128]{0:T(128)S(1)} %slice_reduce_fusion), kind=kLoop, calls=%fused_computation | loop fusion | flops 2097152 | bytes 2114048 | tf_op jit(solution)/shard_map/convert_element_type | solution.py:280
Async XLA Ops:
  0.0 98.0 %copy-start = (f32[4096]{0:T(1024)S(1)}, f32[4096]{0:T(1024)}, u32[]{:S(2)}) copy-start(f32[4096]{0:T(1024)} %param.7) | copy-start | bytes 49156

commit v3 on v2

--- a/solution.py
+++ b/solution.py
@@ -13,13 +13,16 @@
 
 
 def attention_kernel(
-    q_hbm, k_hbm, v_hbm, out, scale,
-    q, k, v, inner, squares, own, load, recv1, tot, recv2, tsum, sib, pbuf, recvy, rbuf, recvx, send3, recv3, send4, fin,
-    s1, r1, s2, r2, ss, rs, sy, ry, sx, rx, s3, r3, s4, r4,
+    q_hbm, k_hbm, v_hbm, gain, out,
+    q, k, v, inner, squares, own, load,
+    ra, psum, rb, ctot, rc, tsum, sib, pbuf, recvy, rbuf, recvx,
+    sendc, enter, sendb, pair_enter, senda, fin,
+    sa, qa, sb, qb, sc, qc, ss, rs, sy, ry, sx, rx, sc2, qc2, sb2, qb2, sa2, qa2,
 ):
     g = lax.axis_index("seq")
     z = lax.axis_index("head")
     a, b = lax.div(z, 4), lax.rem(z, 4)
+    p, e = lax.div(b, 2), lax.rem(b, 2)
     core = lax.rem(g, 2)
     y = lax.rem(lax.div(g, 2), 4)
     x = lax.div(g, 8)
@@ -28,8 +31,9 @@
     def step(v, d):
         return lax.rem(v + d, 4)
 
-    def at_b(d):
-        return {"seq": g, "head": a * 4 + step(b, d)}
+    at_e = {"seq": g, "head": z + 1 - 2 * e}
+    at_p = {"seq": g, "head": z + 2 - 4 * p}
+    at_core = {"seq": other, "head": z}
 
     def at_a(d):
         return {"seq": g, "head": step(a, d) * 4 + b}
@@ -66,8 +70,8 @@
         one.start()
 
     barrier = pltpu.get_barrier_semaphore()
-    peers = [f(d) for f in (at_b, at_a, at_y, at_x) for d in (1, 2, 3)]
-    peers.append({"seq": other, "head": z})
+    peers = [f(d) for f in (at_a, at_y, at_x) for d in (1, 2, 3)]
+    peers.extend([at_e, at_p, at_core])
     for peer in peers:
         pl.semaphore_signal(barrier, inc=1, device_id=peer, device_id_type=MESH)
 
@@ -77,7 +81,7 @@
     def own_states(h):
         def body(j, carry):
             for i in range(4):
-                head = 8 * j + 4 * h + i
+                head = 16 * h + 4 * j + i
                 state = lax.dot_general(
                     k[:, cols(head)], v[:, cols(head)], (((0,), (0,)), ((), ())),
                     preferred_element_type=F32,
@@ -109,7 +113,7 @@
         def body(j, carry):
             total = squares[...]
             for i in range(4):
-                head = 8 * j + 4 * h + i
+                head = 16 * h + 4 * j + i
                 at = cols(head)
                 outer = jnp.dot(q[:, at], fin[head], preferred_element_type=F32)
                 attended = (inner[:, at] + outer).astype(BF16)
@@ -126,34 +130,32 @@
     own_states(0)
     pl.semaphore_wait(barrier, len(peers))
 
-    def to_clusters(h):
-        return start([
-            copy(own.at[pl.ds(8 * step(b, d) + 4 * h, 4)], recv1.at[h, b],
-                 s1.at[h, d - 1], r1.at[h, d - 1], at_b(d))
-            for d in (1, 3, 2)
-        ])
+    def to_pairs(h):
+        return start([copy(own.at[pl.ds(16 * h + 8 * (1 - e), 8)], ra.at[h], sa.at[h], qa.at[h], at_e)])
+
+    def pair_total(h):
+        for i in range(8):
+            mine = own[16 * h + 8 * e + i].astype(F32)
+            psum[h, i] = (mine + ra[h, i].astype(F32)).astype(BF16)
+        return start([copy(psum.at[h, pl.ds(4 * (1 - p), 4)], rb.at[h], sb.at[h], qb.at[h], at_p)])
 
     def cluster_total(h):
         for i in range(4):
-            mine = own[8 * b + 4 * h + i]
-            recv1[h, b, i] = mine
-            total = recv1[h, 0, i].astype(F32)
-            for s in range(1, 4):
-                total = total + recv1[h, s, i].astype(F32)
-            tot[h, i] = total.astype(BF16)
-        recv2[h, a] = tot[h, a]
-        return start([
-            copy(tot.at[h, step(a, d)], recv2.at[h, a],
-                 s2.at[h, d - 1], r2.at[h, d - 1], at_a(d))
+            total = psum[h, 4 * p + i].astype(F32) + rb[h, i].astype(F32)
+            ctot[h, i] = total.astype(BF16)
+        rc[h, a] = ctot[h, a]
+        return start([
+            copy(ctot.at[h, step(a, d)], rc.at[h, a],
+                 sc.at[h, d - 1], qc.at[h, d - 1], at_a(d))
             for d in (2, 1, 3)
         ])
 
     def group_total(h):
-        total = recv2[h, 0].astype(F32)
+        total = rc[h, 0].astype(F32)
         for s in range(1, 4):
-            total = total + recv2[h, s].astype(F32)
+            total = total + rc[h, s].astype(F32)
         tsum[h] = total.astype(BF16)
-        return start([copy(tsum.at[h], sib.at[h], ss.at[h], rs.at[h], {"seq": other, "head": z})])
+        return start([copy(tsum.at[h], sib.at[h], ss.at[h], rs.at[h], at_core)])
 
     def chip_total(h):
         both = (tsum[h].astype(F32) + sib[h].astype(F32)).astype(BF16)
@@ -183,45 +185,57 @@
         for s in range(3):
             state = state + jnp.where(s < x, recvx[h, s].astype(F32), 0.0)
         for s in range(4):
-            send3[h, s] = state.astype(BF16)
+            sendc[h, s] = state.astype(BF16)
             if s < 3:
-                state = state + recv2[h, s].astype(F32)
-        recv3[h, a] = send3[h, a]
-        return start([
-            copy(send3.at[h, step(a, d)], recv3.at[h, a],
-                 s3.at[h, d - 1], r3.at[h, d - 1], at_a(d))
+                state = state + rc[h, s].astype(F32)
+        enter[h, a] = sendc[h, a]
+        return start([
+            copy(sendc.at[h, step(a, d)], enter.at[h, a],
+                 sc2.at[h, d - 1], qc2.at[h, d - 1], at_a(d))
             for d in (2, 1, 3)
         ])
 
-    def to_blocks(h):
+    def back_to_pairs(h):
         for i in range(4):
-            state = recv3[h, i].astype(F32)
-            for s in range(4):
-                send4[h, s, i] = state.astype(BF16)
-                if s < 3:
-                    state = state + recv1[h, s, i].astype(F32)
-        mine = pl.ds(8 * b + 4 * h, 4)
-        fin[mine] = send4[h, b]
-        return start([
-            copy(send4.at[h, step(b, d)], fin.at[mine],
-                 s4.at[h, d - 1], r4.at[h, d - 1], at_b(d))
-            for d in (1, 3, 2)
-        ])
-
-    c1 = [to_clusters(0)]
+            state = enter[h, i].astype(F32)
+            first = psum[h, 4 * p + i].astype(F32)
+            sendb[h, i] = (state + jnp.where(p == 0, first, 0.0)).astype(BF16)
+            second = rb[h, i].astype(F32)
+            pair_enter[h, 4 * p + i] = (state + jnp.where(p == 1, second, 0.0)).astype(BF16)
+        return start([
+            copy(sendb.at[h], pair_enter.at[h, pl.ds(4 * p, 4)], sb2.at[h], qb2.at[h], at_p)
+        ])
+
+    def back_to_blocks(h):
+        for i in range(8):
+            head = 16 * h + 8 * e + i
+            state = pair_enter[h, i].astype(F32)
+            first = own[head].astype(F32)
+            senda[h, i] = (state + jnp.where(e == 0, first, 0.0)).astype(BF16)
+            second = ra[h, i].astype(F32)
+            fin[head] = (state + jnp.where(e == 1, second, 0.0)).astype(BF16)
+        return start([
+            copy(senda.at[h], fin.at[pl.ds(16 * h + 8 * e, 8)], sa2.at[h], qa2.at[h], at_e)
+        ])
+
+    ca0 = to_pairs(0)
     own_states(1)
-    c1.append(to_clusters(1))
+    ca1 = to_pairs(1)
+    arrive(ca0)
+    cb0 = pair_total(0)
     loads[2].wait()
     inner_products()
-    arrive(c1[0])
-    c20 = cluster_total(0)
-    arrive(c1[1])
-    c21 = cluster_total(1)
-    arrive(c20)
+    arrive(ca1)
+    cb1 = pair_total(1)
+    arrive(cb0)
+    cc0 = cluster_total(0)
+    arrive(cb1)
+    cc1 = cluster_total(1)
+    arrive(cc0)
     cs0 = group_total(0)
     arrive(cs0)
     cy0 = chip_total(0)
-    arrive(c21)
+    arrive(cc1)
     cs1 = group_total(1)
     arrive(cy0)
     cx0 = row_total(0)
@@ -234,15 +248,27 @@
     arrive(cx1)
     c31 = earlier_groups(1)
     arrive(c30)
-    c40 = to_blocks(0)
+    cp0 = back_to_pairs(0)
     arrive(c31)
-    c41 = to_blocks(1)
+    cp1 = back_to_pairs(1)
+    arrive(cp0)
+    c40 = back_to_blocks(0)
+    arrive(cp1)
+    c41 = back_to_blocks(1)
     arrive(c40)
     outer_products(0)
     arrive(c41)
     outer_products(1)
     meansq = jnp.sum(squares[...], axis=1, keepdims=True) * (1.0 / (HEADS * E))
-    scale[...] = jnp.broadcast_to(lax.rsqrt(meansq + 1e-06), scale.shape)
+    scale = lax.rsqrt(meansq + 1e-06)
+
+    def norm(j, carry):
+        for i in range(4):
+            at = cols(4 * j + i)
+            out[:, at] = (out[:, at].astype(F32) * scale * gain[:, at]).astype(BF16)
+        return carry
+
+    lax.fori_loop(0, HEADS // 4, norm, 0)
     for one in started:
         one.wait_send()
 
@@ -254,30 +280,28 @@
         return pltpu.VMEM((*lead, E, E), BF16)
 
     dma = pltpu.SemaphoreType.DMA
+    one = [dma((2,)), dma((2,))]
     three = [dma((2, 3)), dma((2, 3))]
     vmem = pl.BlockSpec(memory_space=pltpu.VMEM)
     hbm = pl.BlockSpec(memory_space=pltpu.HBM)
     tokens = pltpu.VMEM((rows, feat), BF16)
-    attended, scale = pl.pallas_call(
+    return pl.pallas_call(
         attention_kernel,
-        out_shape=(
-            jax.ShapeDtypeStruct((rows, feat), BF16),
-            jax.ShapeDtypeStruct((rows, E), F32),
-        ),
-        in_specs=[hbm] * 3,
-        out_specs=(vmem, vmem),
+        out_shape=jax.ShapeDtypeStruct((rows, feat), BF16),
+        in_specs=[hbm, hbm, hbm, vmem],
+        out_specs=vmem,
         scratch_shapes=[
             tokens, tokens, tokens, pltpu.VMEM((rows, feat), F32), pltpu.VMEM((rows, E), F32),
             buf(HEADS), dma((3,)),
-            buf(2, 4, 4), buf(2, 4), buf(2, 4), buf(2), buf(2), buf(2), buf(2, 4), buf(2),
-            buf(2, 4), buf(2, 4), buf(2, 4), buf(2, 4, 4), buf(HEADS),
-            *three, *three, dma((2,)), dma((2,)), *three, *three, *three, *three,
+            buf(2, 8), buf(2, 8), buf(2, 4), buf(2, 4), buf(2, 4),
+            buf(2), buf(2), buf(2), buf(2, 4), buf(2), buf(2, 4),
+            buf(2, 4), buf(2, 4), buf(2, 4), buf(2, 8), buf(2, 8), buf(HEADS),
+            *one, *one, *three, *one, *three, *three, *three, *one, *one,
         ],
         compiler_params=pltpu.CompilerParams(
             collective_id=0, has_side_effects=True, vmem_limit_bytes=65600000
         ),
-    )(queries, keys, values)
-    return (attended.astype(F32) * scale[:, :1] * gain[None, :]).astype(BF16)
+    )(queries, keys, values, gain.reshape(1, feat))
 
 
 def solution(mesh):

time: 101 us -> 96.5 us (0.955); the launches traced: 101 us -> 94.8 us
  Pallas kernels: 97 us -> 92.5 us
  other arithmetic: 2.52 us -> 0 us
  local copies, waits for them, and re-layouts: 0.95 us -> 2.29 us
    pallas_call x1, Pallas kernels: 97 us -> 92.5 us  [per_device(): pl.pallas_call(attention_kernel, out_shape=jax.ShapeDtypeStruct((rows, fe...]
    convert_element_type x1 -> x0, other arithmetic: 2.52 us -> none  [per_device(): return (attended.astype(F32) * scale[:, :1] * gain[None, :]).astype(BF16)]
    unnamed x2 -> x1, local copies, waits for them, and re-layouts: 0.01 us -> 2.29 us
where the time goes in v3:
time: 96.5 us; the launch traced here: 94.8 us
  Pallas kernels  92.5 us (96%)
  local copies, waits for them, and re-layouts  2.29 us (2%)
    pallas_call x1, Pallas kernels, per_device(): pl.pallas_call(attention_kernel, out_shape=jax.ShapeDtypeStruct((rows, fe...  92.5 us
    unnamed x1, local copies, waits for them, and re-layouts  2.29 us

profile of v3, /device:TPU:1, one launch (start us, length us, event | category | flops | bytes accessed | tf_op | source)
XLA Modules:
  0.0 94.8 jit_solution(17602784886765681779)
XLA Ops:
  0.0 92.5 %shard_map.46 = bf16[128,4096]{1,0:T(8,128)(2,1)} custom-call(bf16[128,4096]{1,0:T(8,128)(2,1)} %q_hbm.1, bf16[128,4096]{1,0:T(8,128)(2,1)} %k_hbm.1, bf16[128,4096]{1,0:T(8,128)(2,1)} %v_hbm.1, f32[1,4096]{1,0:T(1,128)} %bitcast.1), custom_call_target="tpu_custom_call" | custom-call | tf_op jit(solution)/shard_map/pallas_call | solution.py:288
  92.5 2.3 %copy.6 = bf16[128,4096]{1,0:T(8,128)(2,1)} copy(bf16[128,4096]{1,0:T(8,128)(2,1)} %shard_map.46) | data formatting | bytes 2097152

commit v4 on v3

--- a/solution.py
+++ b/solution.py
@@ -7,6 +7,8 @@
 
 E = 128
 HEADS = 32
+PIECES = 4
+ROWS = 64
 F32 = jnp.float32
 BF16 = jnp.bfloat16
 MESH = pl.DeviceIdType.MESH
@@ -62,43 +64,45 @@
         for one in copies:
             one.wait_recv()
 
-    loads = [
-        pltpu.make_async_copy(src, dst, load.at[i])
-        for i, (src, dst) in enumerate(((k_hbm, k), (v_hbm, v), (q_hbm, q)))
-    ]
-    for one in loads:
-        one.start()
-
     barrier = pltpu.get_barrier_semaphore()
     peers = [f(d) for f in (at_a, at_y, at_x) for d in (1, 2, 3)]
     peers.extend([at_e, at_p, at_core])
     for peer in peers:
         pl.semaphore_signal(barrier, inc=1, device_id=peer, device_id_type=MESH)
 
+    wide = 8 * E
+    loads = [
+        pltpu.make_async_copy(
+            src.at[:, pl.ds(h * wide, wide)], dst.at[:, pl.ds(h * wide, wide)], load.at[2 * h + i]
+        )
+        for h in range(PIECES)
+        for i, (src, dst) in enumerate(((k_hbm, k), (v_hbm, v)))
+    ]
+    loads.append(pltpu.make_async_copy(q_hbm, q, load.at[2 * PIECES]))
+    for one in loads:
+        one.start()
+
     def cols(head):
         return pl.ds(pl.multiple_of(head * E, E), E)
 
     def own_states(h):
-        def body(j, carry):
-            for i in range(4):
-                head = 16 * h + 4 * j + i
-                state = lax.dot_general(
-                    k[:, cols(head)], v[:, cols(head)], (((0,), (0,)), ((), ())),
-                    preferred_element_type=F32,
-                )
-                own[head] = state.astype(BF16)
-            return carry
-
-        lax.fori_loop(0, 4, body, 0)
-
-    def inner_products():
+        loads[2 * h].wait()
+        loads[2 * h + 1].wait()
+        for head in range(8 * h, 8 * h + 8):
+            at = pl.ds(head * E, E)
+            state = lax.dot_general(
+                k[:, at], v[:, at], (((0,), (0,)), ((), ())), preferred_element_type=F32
+            )
+            own[pl.ds(2 * head, 2)] = state.astype(BF16).reshape(2, ROWS, E)
+
+    def inner_products(h):
         lower = lax.broadcasted_iota(jnp.int32, (E, E), 0) >= lax.broadcasted_iota(
             jnp.int32, (E, E), 1
         )
 
         def body(j, carry):
             for i in range(4):
-                at = cols(4 * j + i)
+                at = cols(8 * h + 4 * j + i)
                 scores = lax.dot_general(
                     q[:, at], k[:, at], (((1,), (1,)), ((), ())), preferred_element_type=F32
                 )
@@ -106,16 +110,16 @@
                 inner[:, at] = jnp.dot(scores, v[:, at], preferred_element_type=F32)
             return carry
 
-        lax.fori_loop(0, HEADS // 4, body, 0)
-        squares[...] = jnp.zeros_like(squares)
+        lax.fori_loop(0, 2, body, 0)
 
     def outer_products(h):
         def body(j, carry):
             total = squares[...]
             for i in range(4):
-                head = 16 * h + 4 * j + i
+                head = 8 * h + 4 * j + i
                 at = cols(head)
-                outer = jnp.dot(q[:, at], fin[head], preferred_element_type=F32)
+                state = fin[pl.ds(2 * head, 2)].reshape(E, E)
+                outer = jnp.dot(q[:, at], state, preferred_element_type=F32)
                 attended = (inner[:, at] + outer).astype(BF16)
                 out[:, at] = attended
                 wide = attended.astype(F32)
@@ -123,10 +127,8 @@
             squares[...] = total
             return carry
 
-        lax.fori_loop(0, 4, body, 0)
-
-    loads[0].wait()
-    loads[1].wait()
+        lax.fori_loop(0, 2, body, 0)
+
     own_states(0)
     pl.semaphore_wait(barrier, len(peers))
 
@@ -218,47 +220,28 @@
             copy(senda.at[h], fin.at[pl.ds(16 * h + 8 * e, 8)], sa2.at[h], qa2.at[h], at_e)
         ])
 
-    ca0 = to_pairs(0)
+    steps = [
+        (pair_total, 4.5), (cluster_total, 10.0), (group_total, 19.0), (chip_total, 21.0),
+        (row_total, 24.0), (earlier_groups, 27.5), (back_to_pairs, 36.5),
+        (back_to_blocks, 42.0), (outer_products, 47.0),
+    ]
+    order = sorted(
+        (when + 4.0 * h, h, n) for n, (_, when) in enumerate(steps) for h in range(PIECES)
+    )
+    flying = {0: to_pairs(0)}
     own_states(1)
-    ca1 = to_pairs(1)
-    arrive(ca0)
-    cb0 = pair_total(0)
-    loads[2].wait()
-    inner_products()
-    arrive(ca1)
-    cb1 = pair_total(1)
-    arrive(cb0)
-    cc0 = cluster_total(0)
-    arrive(cb1)
-    cc1 = cluster_total(1)
-    arrive(cc0)
-    cs0 = group_total(0)
-    arrive(cs0)
-    cy0 = chip_total(0)
-    arrive(cc1)
-    cs1 = group_total(1)
-    arrive(cy0)
-    cx0 = row_total(0)
-    arrive(cs1)
-    cy1 = chip_total(1)
-    arrive(cx0)
-    c30 = earlier_groups(0)
-    arrive(cy1)
-    cx1 = row_total(1)
-    arrive(cx1)
-    c31 = earlier_groups(1)
-    arrive(c30)
-    cp0 = back_to_pairs(0)
-    arrive(c31)
-    cp1 = back_to_pairs(1)
-    arrive(cp0)
-    c40 = back_to_blocks(0)
-    arrive(cp1)
-    c41 = back_to_blocks(1)
-    arrive(c40)
-    outer_products(0)
-    arrive(c41)
-    outer_products(1)
+    flying[1] = to_pairs(1)
+    own_states(2)
+    own_states(3)
+    squares[...] = jnp.zeros_like(squares)
+    loads[-1].wait()
+    for _, h, n in order:
+        arrive(flying[h])
+        flying[h] = steps[n][0](h)
+        if n == 0:
+            if h + 2 < PIECES:
+                flying[h + 2] = to_pairs(h + 2)
+            inner_products(h)
     meansq = jnp.sum(squares[...], axis=1, keepdims=True) * (1.0 / (HEADS * E))
     scale = lax.rsqrt(meansq + 1e-06)
 
@@ -277,11 +260,12 @@
     rows, feat = queries.shape
 
     def buf(*lead):
-        return pltpu.VMEM((*lead, E, E), BF16)
+        return pltpu.VMEM((*lead, ROWS, E), BF16)
 
     dma = pltpu.SemaphoreType.DMA
-    one = [dma((2,)), dma((2,))]
-    three = [dma((2, 3)), dma((2, 3))]
+    n = PIECES
+    one = [dma((n,)), dma((n,))]
+    three = [dma((n, 3)), dma((n, 3))]
     vmem = pl.BlockSpec(memory_space=pltpu.VMEM)
     hbm = pl.BlockSpec(memory_space=pltpu.HBM)
     tokens = pltpu.VMEM((rows, feat), BF16)
@@ -292,10 +276,10 @@
         out_specs=vmem,
         scratch_shapes=[
             tokens, tokens, tokens, pltpu.VMEM((rows, feat), F32), pltpu.VMEM((rows, E), F32),
-            buf(HEADS), dma((3,)),
-            buf(2, 8), buf(2, 8), buf(2, 4), buf(2, 4), buf(2, 4),
-            buf(2), buf(2), buf(2), buf(2, 4), buf(2), buf(2, 4),
-            buf(2, 4), buf(2, 4), buf(2, 4), buf(2, 8), buf(2, 8), buf(HEADS),
+            buf(2 * HEADS), dma((2 * PIECES + 1,)),
+            buf(n, 8), buf(n, 8), buf(n, 4), buf(n, 4), buf(n, 4),
+            buf(n), buf(n), buf(n), buf(n, 4), buf(n), buf(n, 4),
+            buf(n, 4), buf(n, 4), buf(n, 4), buf(n, 8), buf(n, 8), buf(2 * HEADS),
             *one, *one, *three, *one, *three, *three, *three, *one, *one,
         ],
         compiler_params=pltpu.CompilerParams(

time: 96.5 us -> 90.3 us (0.936)
  Pallas kernels: 92.5 us -> 86.9 us
    pallas_call x1, Pallas kernels: 92.5 us -> 86.9 us  [per_device(): pl.pallas_call(attention_kernel, out_shape=jax.ShapeDtypeStruct((rows, fe...]
where the time goes in v4:
time: 90.3 us; the launch traced here: 89.2 us
  Pallas kernels  86.9 us (96%)
  local copies, waits for them, and re-layouts  2.29 us (3%)
    pallas_call x1, Pallas kernels, per_device(): pl.pallas_call(attention_kernel, out_shape=jax.ShapeDtypeStruct((rows, fe...  86.9 us
    unnamed x1, local copies, waits for them, and re-layouts  2.29 us

profile of v4, /device:TPU:1, one launch (start us, length us, event | category | flops | bytes accessed | tf_op | source)
XLA Modules:
  0.0 89.2 jit_solution(9279865296596440992)
XLA Ops:
  0.0 86.9 %shard_map.46 = bf16[128,4096]{1,0:T(8,128)(2,1)} custom-call(bf16[128,4096]{1,0:T(8,128)(2,1)} %q_hbm.1, bf16[128,4096]{1,0:T(8,128)(2,1)} %k_hbm.1, bf16[128,4096]{1,0:T(8,128)(2,1)} %v_hbm.1, f32[1,4096]{1,0:T(1,128)} %bitcast.1), custom_call_target="tpu_custom_call" | custom-call | tf_op jit(solution)/shard_map/pallas_call | solution.py:272
  86.9 2.3 %copy.6 = bf16[128,4096]{1,0:T(8,128)(2,1)} copy(bf16[128,4096]{1,0:T(8,128)(2,1)} %shard_map.46) | data formatting | bytes 2097152

commit v5 on v4

--- a/solution.py
+++ b/solution.py
@@ -15,36 +15,34 @@
 
 
 def attention_kernel(
-    q_hbm, k_hbm, v_hbm, gain, out,
-    q, k, v, inner, squares, own, load,
-    ra, psum, rb, ctot, rc, tsum, sib, pbuf, recvy, rbuf, recvx,
+    q_hbm, k_hbm, v_hbm, out_hbm,
+    q, k, v, inner, out, own, load, leave,
+    ra, psum, rb, ctot, rc, tsum, recvy, rbuf, recvx,
     sendc, enter, sendb, pair_enter, senda, fin,
-    sa, qa, sb, qb, sc, qc, ss, rs, sy, ry, sx, rx, sc2, qc2, sb2, qb2, sa2, qa2,
+    sa, qa, sb, qb, sc, qc, sy, ry, sx, rx, sc2, qc2, sb2, qb2, sa2, qa2,
 ):
     g = lax.axis_index("seq")
     z = lax.axis_index("head")
     a, b = lax.div(z, 4), lax.rem(z, 4)
     p, e = lax.div(b, 2), lax.rem(b, 2)
-    core = lax.rem(g, 2)
-    y = lax.rem(lax.div(g, 2), 4)
     x = lax.div(g, 8)
-    other = g + 1 - 2 * core
 
     def step(v, d):
         return lax.rem(v + d, 4)
 
     at_e = {"seq": g, "head": z + 1 - 2 * e}
     at_p = {"seq": g, "head": z + 2 - 4 * p}
-    at_core = {"seq": other, "head": z}
 
     def at_a(d):
         return {"seq": g, "head": step(a, d) * 4 + b}
 
-    def at_y(d):
-        return {"seq": x * 8 + step(y, d) * 2 + core, "head": z}
+    row_at = lax.rem(g, 8)
+
+    def at_row(d):
+        return {"seq": x * 8 + lax.rem(row_at + d, 8), "head": z}
 
     def at_x(d):
-        return {"seq": step(x, d) * 8 + y * 2 + core, "head": z}
+        return {"seq": step(x, d) * 8 + row_at, "head": z}
 
     def copy(src, dst, send, recv, where):
         return pltpu.make_async_remote_copy(
@@ -65,8 +63,9 @@
             one.wait_recv()
 
     barrier = pltpu.get_barrier_semaphore()
-    peers = [f(d) for f in (at_a, at_y, at_x) for d in (1, 2, 3)]
-    peers.extend([at_e, at_p, at_core])
+    peers = [f(d) for f in (at_a, at_x) for d in (1, 2, 3)]
+    peers.extend([at_e, at_p])
+    peers.extend(at_row(d) for d in range(1, 8))
     for peer in peers:
         pl.semaphore_signal(barrier, inc=1, device_id=peer, device_id_type=MESH)
 
@@ -114,20 +113,19 @@
 
     def outer_products(h):
         def body(j, carry):
-            total = squares[...]
             for i in range(4):
                 head = 8 * h + 4 * j + i
                 at = cols(head)
                 state = fin[pl.ds(2 * head, 2)].reshape(E, E)
                 outer = jnp.dot(q[:, at], state, preferred_element_type=F32)
-                attended = (inner[:, at] + outer).astype(BF16)
-                out[:, at] = attended
-                wide = attended.astype(F32)
-                total = total + wide * wide
-            squares[...] = total
+                out[:, at] = (inner[:, at] + outer).astype(BF16)
             return carry
 
         lax.fori_loop(0, 2, body, 0)
+        mine = pl.ds(h * wide, wide)
+        leaving = pltpu.make_async_copy(out.at[:, mine], out_hbm.at[:, mine], leave.at[h])
+        leaving.start()
+        return leaving
 
     own_states(0)
     pl.semaphore_wait(barrier, len(peers))
@@ -156,21 +154,17 @@
         total = rc[h, 0].astype(F32)
         for s in range(1, 4):
             total = total + rc[h, s].astype(F32)
-        tsum[h] = total.astype(BF16)
-        return start([copy(tsum.at[h], sib.at[h], ss.at[h], rs.at[h], at_core)])
-
-    def chip_total(h):
-        both = (tsum[h].astype(F32) + sib[h].astype(F32)).astype(BF16)
-        pbuf[h] = both
-        recvy[h, y] = both
-        return start([
-            copy(pbuf.at[h], recvy.at[h, y], sy.at[h, d - 1], ry.at[h, d - 1], at_y(d))
-            for d in (2, 1, 3)
+        group = total.astype(BF16)
+        tsum[h] = group
+        recvy[h, row_at] = group
+        return start([
+            copy(tsum.at[h], recvy.at[h, row_at], sy.at[h, d - 1], ry.at[h, d - 1], at_row(d))
+            for d in (4, 3, 5, 2, 6, 1, 7)
         ])
 
     def row_total(h):
         total = recvy[h, 0].astype(F32)
-        for s in range(1, 4):
+        for s in range(1, 8):
             total = total + recvy[h, s].astype(F32)
         row = total.astype(BF16)
         rbuf[h] = row
@@ -181,9 +175,9 @@
         ])
 
     def earlier_groups(h):
-        state = jnp.where(core == 1, sib[h].astype(F32), 0.0)
-        for s in range(3):
-            state = state + jnp.where(s < y, recvy[h, s].astype(F32), 0.0)
+        state = jnp.where(row_at > 0, recvy[h, 0].astype(F32), 0.0)
+        for s in range(1, 7):
+            state = state + jnp.where(s < row_at, recvy[h, s].astype(F32), 0.0)
         for s in range(3):
             state = state + jnp.where(s < x, recvx[h, s].astype(F32), 0.0)
         for s in range(4):
@@ -221,9 +215,9 @@
         ])
 
     steps = [
-        (pair_total, 4.5), (cluster_total, 10.0), (group_total, 19.0), (chip_total, 21.0),
-        (row_total, 24.0), (earlier_groups, 27.5), (back_to_pairs, 36.5),
-        (back_to_blocks, 42.0), (outer_products, 47.0),
+        (pair_total, 4.5), (cluster_total, 10.0), (group_total, 19.0), (row_total, 22.5),
+        (earlier_groups, 26.0), (back_to_pairs, 35.0), (back_to_blocks, 40.5),
+        (outer_products, 45.5),
     ]
     order = sorted(
         (when + 4.0 * h, h, n) for n, (_, when) in enumerate(steps) for h in range(PIECES)
@@ -233,7 +227,6 @@
     flying[1] = to_pairs(1)
     own_states(2)
     own_states(3)
-    squares[...] = jnp.zeros_like(squares)
     loads[-1].wait()
     for _, h, n in order:
         arrive(flying[h])
@@ -242,18 +235,16 @@
             if h + 2 < PIECES:
                 flying[h + 2] = to_pairs(h + 2)
             inner_products(h)
-    meansq = jnp.sum(squares[...], axis=1, keepdims=True) * (1.0 / (HEADS * E))
-    scale = lax.rsqrt(meansq + 1e-06)
-
-    def norm(j, carry):
-        for i in range(4):
-            at = cols(4 * j + i)
-            out[:, at] = (out[:, at].astype(F32) * scale * gain[:, at]).astype(BF16)
-        return carry
-
-    lax.fori_loop(0, HEADS // 4, norm, 0)
     for one in started:
         one.wait_send()
+    for h in range(PIECES):
+        flying[h].wait()
+
+
+def norm_kernel(attended, gain, out):
+    wide = attended[...].astype(F32)
+    meansq = jnp.mean(wide * wide, axis=1, keepdims=True)
+    out[...] = (wide * lax.rsqrt(meansq + 1e-06) * gain[...]).astype(BF16)
 
 
 def per_device(queries, keys, values, gain):
@@ -266,26 +257,36 @@
     n = PIECES
     one = [dma((n,)), dma((n,))]
     three = [dma((n, 3)), dma((n, 3))]
-    vmem = pl.BlockSpec(memory_space=pltpu.VMEM)
+    seven = [dma((n, 7)), dma((n, 7))]
     hbm = pl.BlockSpec(memory_space=pltpu.HBM)
     tokens = pltpu.VMEM((rows, feat), BF16)
-    return pl.pallas_call(
+    attended = pl.pallas_call(
         attention_kernel,
         out_shape=jax.ShapeDtypeStruct((rows, feat), BF16),
-        in_specs=[hbm, hbm, hbm, vmem],
-        out_specs=vmem,
+        in_specs=[hbm, hbm, hbm],
+        out_specs=hbm,
         scratch_shapes=[
-            tokens, tokens, tokens, pltpu.VMEM((rows, feat), F32), pltpu.VMEM((rows, E), F32),
-            buf(2 * HEADS), dma((2 * PIECES + 1,)),
+            tokens, tokens, tokens, pltpu.VMEM((rows, feat), F32), tokens,
+            buf(2 * HEADS), dma((2 * PIECES + 1,)), dma((n,)),
             buf(n, 8), buf(n, 8), buf(n, 4), buf(n, 4), buf(n, 4),
-            buf(n), buf(n), buf(n), buf(n, 4), buf(n), buf(n, 4),
+            buf(n), buf(n, 8), buf(n), buf(n, 4),
             buf(n, 4), buf(n, 4), buf(n, 4), buf(n, 8), buf(n, 8), buf(2 * HEADS),
-            *one, *one, *three, *one, *three, *three, *three, *one, *one,
+            *one, *one, *three, *seven, *three, *three, *one, *one,
         ],
         compiler_params=pltpu.CompilerParams(
             collective_id=0, has_side_effects=True, vmem_limit_bytes=65600000
         ),
-    )(queries, keys, values, gain.reshape(1, feat))
+    )(queries, keys, values)
+    return pl.pallas_call(
+        norm_kernel,
+        out_shape=jax.ShapeDtypeStruct((rows, feat), BF16),
+        grid=(4,),
+        in_specs=[
+            pl.BlockSpec((rows // 4, feat), lambda i: (i, 0)),
+            pl.BlockSpec((1, feat), lambda i: (0, 0)),
+        ],
+        out_specs=pl.BlockSpec((rows // 4, feat), lambda i: (i, 0)),
+    )(attended, gain.reshape(1, feat))
 
 
 def solution(mesh):

time: 90.3 us -> 90.8 us (level)
  local copies, waits for them, and re-layouts: 2.29 us -> 0 us
  Pallas kernels: 86.9 us -> 89.1 us
    pallas_call x0 -> x1, Pallas kernels: none -> 3.68 us  [per_device(): pl.pallas_call(norm_kernel, out_shape=jax.ShapeDtypeStruct((rows, feat),...]
    unnamed x1 -> x0, local copies, waits for them, and re-layouts: 2.29 us -> none
    pallas_call x1, Pallas kernels: 86.9 us -> 85.4 us  [per_device(): pl.pallas_call(attention_kernel, out_shape=jax.ShapeDtypeStruct((rows, fe...]
where the time goes in v5:
time: 90.8 us; the launch traced here: 89.1 us
  Pallas kernels  89.1 us (98%)
    pallas_call x1, Pallas kernels, per_device(): pl.pallas_call(attention_kernel, out_shape=jax.ShapeDtypeStruct((rows, fe...  85.4 us
    pallas_call x1, Pallas kernels, per_device(): pl.pallas_call(norm_kernel, out_shape=jax.ShapeDtypeStruct((rows, feat),...  3.68 us

profile of v5, /device:TPU:1, one launch (start us, length us, event | category | flops | bytes accessed | tf_op | source)
XLA Modules:
  0.0 89.1 jit_solution(2272444222428205218)
XLA Ops:
  0.0 85.4 %shard_map.46.attended = bf16[128,4096]{1,0:T(8,128)(2,1)} custom-call(bf16[128,4096]{1,0:T(8,128)(2,1)} %q_hbm.1, bf16[128,4096]{1,0:T(8,128)(2,1)} %k_hbm.1, bf16[128,4096]{1,0:T(8,128)(2,1)} %v_hbm.1), custom_call_target="tpu_custom_call" | custom-call | tf_op jit(solution)/shard_map/pallas_call | solution.py:263
  85.4 3.7 %shard_map.47 = bf16[128,4096]{1,0:T(8,128)(2,1)} custom-call(bf16[128,4096]{1,0:T(8,128)(2,1)} %shard_map.46.attended, f32[1,4096]{1,0:T(1,128)} %bitcast.1), custom_call_target="tpu_custom_call" | custom-call | tf_op jit(solution)/shard_map/pallas_call | solution.py:280

commit v6 on v5

--- a/solution.py
+++ b/solution.py
@@ -9,14 +9,16 @@
 HEADS = 32
 PIECES = 4
 ROWS = 64
+AHEAD = 2
+APART = 4.0
 F32 = jnp.float32
 BF16 = jnp.bfloat16
 MESH = pl.DeviceIdType.MESH
 
 
 def attention_kernel(
-    q_hbm, k_hbm, v_hbm, out_hbm,
-    q, k, v, inner, out, own, load, leave,
+    q_hbm, k_hbm, v_hbm, gain, out,
+    q, k, v, inner, squares, own, load,
     ra, psum, rb, ctot, rc, tsum, recvy, rbuf, recvx,
     sendc, enter, sendb, pair_enter, senda, fin,
     sa, qa, sb, qb, sc, qc, sy, ry, sx, rx, sc2, qc2, sb2, qb2, sa2, qa2,
@@ -113,19 +115,20 @@
 
     def outer_products(h):
         def body(j, carry):
+            total = squares[...]
             for i in range(4):
                 head = 8 * h + 4 * j + i
                 at = cols(head)
                 state = fin[pl.ds(2 * head, 2)].reshape(E, E)
                 outer = jnp.dot(q[:, at], state, preferred_element_type=F32)
-                out[:, at] = (inner[:, at] + outer).astype(BF16)
+                attended = (inner[:, at] + outer).astype(BF16)
+                out[:, at] = attended
+                wide = attended.astype(F32)
+                total = total + wide * wide
+            squares[...] = total
             return carry
 
         lax.fori_loop(0, 2, body, 0)
-        mine = pl.ds(h * wide, wide)
-        leaving = pltpu.make_async_copy(out.at[:, mine], out_hbm.at[:, mine], leave.at[h])
-        leaving.start()
-        return leaving
 
     own_states(0)
     pl.semaphore_wait(barrier, len(peers))
@@ -220,31 +223,34 @@
         (outer_products, 45.5),
     ]
     order = sorted(
-        (when + 4.0 * h, h, n) for n, (_, when) in enumerate(steps) for h in range(PIECES)
+        (when + APART * h, h, n) for n, (_, when) in enumerate(steps) for h in range(PIECES)
     )
     flying = {0: to_pairs(0)}
-    own_states(1)
-    flying[1] = to_pairs(1)
-    own_states(2)
-    own_states(3)
+    for h in range(1, PIECES):
+        own_states(h)
+        if h < AHEAD:
+            flying[h] = to_pairs(h)
+    squares[...] = jnp.zeros_like(squares)
     loads[-1].wait()
     for _, h, n in order:
         arrive(flying[h])
         flying[h] = steps[n][0](h)
         if n == 0:
-            if h + 2 < PIECES:
-                flying[h + 2] = to_pairs(h + 2)
+            if h + AHEAD < PIECES:
+                flying[h + AHEAD] = to_pairs(h + AHEAD)
             inner_products(h)
+    meansq = jnp.sum(squares[...], axis=1, keepdims=True) * (1.0 / (HEADS * E))
+    scale = lax.rsqrt(meansq + 1e-06)
+
+    def norm(j, carry):
+        for i in range(4):
+            at = cols(4 * j + i)
+            out[:, at] = (out[:, at].astype(F32) * scale * gain[:, at]).astype(BF16)
+        return carry
+
+    lax.fori_loop(0, HEADS // 4, norm, 0)
     for one in started:
         one.wait_send()
-    for h in range(PIECES):
-        flying[h].wait()
-
-
-def norm_kernel(attended, gain, out):
-    wide = attended[...].astype(F32)
-    meansq = jnp.mean(wide * wide, axis=1, keepdims=True)
-    out[...] = (wide * lax.rsqrt(meansq + 1e-06) * gain[...]).astype(BF16)
 
 
 def per_device(queries, keys, values, gain):
@@ -259,15 +265,16 @@
     three = [dma((n, 3)), dma((n, 3))]
     seven = [dma((n, 7)), dma((n, 7))]
     hbm = pl.BlockSpec(memory_space=pltpu.HBM)
+    vmem = pl.BlockSpec(memory_space=pltpu.VMEM)
     tokens = pltpu.VMEM((rows, feat), BF16)
-    attended = pl.pallas_call(
+    return pl.pallas_call(
         attention_kernel,
         out_shape=jax.ShapeDtypeStruct((rows, feat), BF16),
-        in_specs=[hbm, hbm, hbm],
-        out_specs=hbm,
+        in_specs=[hbm, hbm, hbm, vmem],
+        out_specs=vmem,
         scratch_shapes=[
-            tokens, tokens, tokens, pltpu.VMEM((rows, feat), F32), tokens,
-            buf(2 * HEADS), dma((2 * PIECES + 1,)), dma((n,)),
+            tokens, tokens, tokens, pltpu.VMEM((rows, feat), F32), pltpu.VMEM((rows, E), F32),
+            buf(2 * HEADS), dma((2 * PIECES + 1,)),
             buf(n, 8), buf(n, 8), buf(n, 4), buf(n, 4), buf(n, 4),
             buf(n), buf(n, 8), buf(n), buf(n, 4),
             buf(n, 4), buf(n, 4), buf(n, 4), buf(n, 8), buf(n, 8), buf(2 * HEADS),
@@ -276,17 +283,7 @@
         compiler_params=pltpu.CompilerParams(
             collective_id=0, has_side_effects=True, vmem_limit_bytes=65600000
         ),
-    )(queries, keys, values)
-    return pl.pallas_call(
-        norm_kernel,
-        out_shape=jax.ShapeDtypeStruct((rows, feat), BF16),
-        grid=(4,),
-        in_specs=[
-            pl.BlockSpec((rows // 4, feat), lambda i: (i, 0)),
-            pl.BlockSpec((1, feat), lambda i: (0, 0)),
-        ],
-        out_specs=pl.BlockSpec((rows // 4, feat), lambda i: (i, 0)),
-    )(attended, gain.reshape(1, feat))
+    )(queries, keys, values, gain.reshape(1, feat))
 
 
 def solution(mesh):

time: 90.8 us -> 90.4 us (level)
  local copies, waits for them, and re-layouts: 0 us -> 2.29 us
  Pallas kernels: 89.1 us -> 87.1 us
    pallas_call x1 -> x0, Pallas kernels: 3.68 us -> none  [per_device(): pl.pallas_call(norm_kernel, out_shape=jax.ShapeDtypeStruct((rows, feat),...]
    unnamed x0 -> x1, local copies, waits for them, and re-layouts: none -> 2.29 us
    pallas_call x1, Pallas kernels: 85.4 us -> 87.1 us  [per_device(): pl.pallas_call(attention_kernel, out_shape=jax.ShapeDtypeStruct((rows, fe...]
where the time goes in v6:
time: 90.4 us; the launch traced here: 89.4 us
  Pallas kernels  87.1 us (96%)
  local copies, waits for them, and re-layouts  2.29 us (3%)
    pallas_call x1, Pallas kernels, per_device(): pl.pallas_call(attention_kernel, out_shape=jax.ShapeDtypeStruct((rows, fe...  87.1 us
    unnamed x1, local copies, waits for them, and re-layouts  2.29 us

profile of v6, /device:TPU:1, one launch (start us, length us, event | category | flops | bytes accessed | tf_op | source)
XLA Modules:
  0.0 89.4 jit_solution(146121399668496486)
XLA Ops:
  0.0 87.1 %shard_map.46 = bf16[128,4096]{1,0:T(8,128)(2,1)} custom-call(bf16[128,4096]{1,0:T(8,128)(2,1)} %q_hbm.1, bf16[128,4096]{1,0:T(8,128)(2,1)} %k_hbm.1, bf16[128,4096]{1,0:T(8,128)(2,1)} %v_hbm.1, f32[1,4096]{1,0:T(1,128)} %bitcast.1), custom_call_target="tpu_custom_call" | custom-call | tf_op jit(solution)/shard_map/pallas_call | solution.py:270
  87.1 2.3 %copy.6 = bf16[128,4096]{1,0:T(8,128)(2,1)} copy(bf16[128,4096]{1,0:T(8,128)(2,1)} %shard_map.46) | data formatting | bytes 2097152

commit v7 on v6

--- a/solution.py
+++ b/solution.py
@@ -9,7 +9,7 @@
 HEADS = 32
 PIECES = 4
 ROWS = 64
-AHEAD = 2
+AHEAD = 3
 APART = 4.0
 F32 = jnp.float32
 BF16 = jnp.bfloat16

time: 90.4 us -> 90.3 us (level)
  no operation moved by 1% of the time
where the time goes in v7:
time: 90.3 us; the launch traced here: 90.1 us
  Pallas kernels  87.8 us (97%)
  local copies, waits for them, and re-layouts  2.29 us (3%)
    pallas_call x1, Pallas kernels, per_device(): pl.pallas_call(attention_kernel, out_shape=jax.ShapeDtypeStruct((rows, fe...  87.8 us
    unnamed x1, local copies, waits for them, and re-layouts  2.29 us

profile of v7, /device:TPU:1, one launch (start us, length us, event | category | flops | bytes accessed | tf_op | source)
XLA Modules:
  0.0 90.1 jit_solution(1828489652067963814)
XLA Ops:
  0.0 87.8 %shard_map.46 = bf16[128,4096]{1,0:T(8,128)(2,1)} custom-call(bf16[128,4096]{1,0:T(8,128)(2,1)} %q_hbm.1, bf16[128,4096]{1,0:T(8,128)(2,1)} %k_hbm.1, bf16[128,4096]{1,0:T(8,128)(2,1)} %v_hbm.1, f32[1,4096]{1,0:T(1,128)} %bitcast.1), custom_call_target="tpu_custom_call" | custom-call | tf_op jit(solution)/shard_map/pallas_call | solution.py:270
  87.8 2.3 %copy.6 = bf16[128,4096]{1,0:T(8,128)(2,1)} copy(bf16[128,4096]{1,0:T(8,128)(2,1)} %shard_map.46) | data formatting | bytes 2097152
